TPU v7x, 32 devices: a whole 2x2x4 slice. The times are simulated.
32 devices in a mesh: dp: 16 (over z, x, core), tensor: 2 (over y).
Axes of the slice: x: 2, y: 2, z: 4, core: 2. Of those that a mesh axis runs over, the one named last changes fastest.
Arguments:
- x_input: bfloat16 [16, 768, 1536], P('dp', 'tensor'), may hold values from -6 to 6
- cond_tokens: bfloat16 [16, 130, 1536], P('dp'), may hold values from -6 to 6
- teacher: bfloat16 [16, 768, 1536], P('dp', 'tensor'), may hold values from -6 to 6
- valid_mask: int32 [16, 768], P('dp', 'tensor'), may hold values from 0 to 1, as said below
- norm_gains: bfloat16 [3, 1536], P(None, 'dp'), may hold values from 0.099609375 to 1.8984375
- w_query: bfloat16 [1536, 1536], P('dp', 'tensor'), may hold values from -0.15625 to 0.15625
- w_key: bfloat16 [1536, 1536], P('dp', 'tensor'), may hold values from -0.15625 to 0.15625
- w_value: bfloat16 [1536, 1536], P('dp', 'tensor'), may hold values from -0.15625 to 0.15625
- w_out: bfloat16 [1536, 1536], P('tensor', 'dp'), may hold values from -3 to 3
- c_query: bfloat16 [1536, 1536], P('dp', 'tensor'), may hold values from -0.15625 to 0.15625
- c_key: bfloat16 [1536, 1536], P('dp', 'tensor'), may hold values from -0.15625 to 0.15625
- c_value: bfloat16 [1536, 1536], P('dp', 'tensor'), may hold values from -0.15625 to 0.15625
- c_out: bfloat16 [1536, 1536], P('tensor', 'dp'), may hold values from -1.25 to 1.25
- w_gate: bfloat16 [1536, 6144], P('dp', 'tensor'), may hold values from -0.15625 to 0.15625
- w_up: bfloat16 [1536, 6144], P('dp', 'tensor'), may hold values from -0.15625 to 0.15625
- w_down: bfloat16 [6144, 1536], P('tensor', 'dp'), may hold values from -0.078125 to 0.078125
Outputs:
- output: bfloat16 [16, 768, 1536], P('dp', 'tensor')
- mean_loss: float32 [], replicated
- grad_input: float32 [16, 768, 1536], P('dp', 'tensor')
- grad_cond: float32 [16, 130, 1536], P('dp')
- grad_w_query: float32 [1536, 1536], P('dp', 'tensor')
- grad_w_key: float32 [1536, 1536], P('dp', 'tensor')
- grad_w_value: float32 [1536, 1536], P('dp', 'tensor')
- grad_w_out: float32 [1536, 1536], P('tensor', 'dp')
- grad_c_query: float32 [1536, 1536], P('dp', 'tensor')
- grad_c_key: float32 [1536, 1536], P('dp', 'tensor')
- grad_c_value: float32 [1536, 1536], P('dp', 'tensor')
- grad_c_out: float32 [1536, 1536], P('tensor', 'dp')
- grad_w_gate: float32 [1536, 6144], P('dp', 'tensor')
- grad_w_up: float32 [1536, 6144], P('dp', 'tensor')
- grad_w_down: float32 [6144, 1536], P('tensor', 'dp')
- grad_norm_gains: float32 [3, 1536], P(None, 'dp')
Inputs may be any that keep to these rules, and one draw needn't show every extreme that they name: `valid_mask`: the valid tokens of each latent form a prefix of it, and every latent has a valid token.
All inputs are finite; a program needn't handle non-finite values.
Results may differ from a plain program's by a relative error of at most 0.017.
Values may be sent and summed in bfloat16 or wider, within the bound.
No kernel may reach another device: no remote copies, remote signals or barrier semaphores. Data moves between devices by JAX's collectives and lax.ppermute only.
A program may use at most 256 MiB of HBM per device.

v0:
```python
import math
import jax
import jax.numpy as jnp
from jax import lax
from jax.sharding import PartitionSpec as P

HEAD_DIM = 64
EPSILON = 1e-05


def matmul(left_side, right_side):
    return jnp.dot(left_side, right_side, preferred_element_type=jnp.float32)


def contract_rows(left_side, right_side):
    return lax.dot_general(
        left_side, right_side, (((0,), (0,)), ((), ())), preferred_element_type=jnp.float32
    )


def times_transposed(left_side, right_side):
    return lax.dot_general(
        left_side, right_side, (((1,), (1,)), ((), ())), preferred_element_type=jnp.float32
    )


def norm_stats(values):
    row_mean = jnp.mean(values, axis=-1, keepdims=True)
    centred = values - row_mean
    row_var = jnp.mean(centred * centred, axis=-1, keepdims=True)
    inverse = lax.rsqrt(row_var + EPSILON)
    return (centred * inverse, inverse)


def norm_back(grad_normed, normed, inverse, gain_row):
    scaled = grad_normed * gain_row
    mean_scaled = jnp.mean(scaled, axis=-1, keepdims=True)
    mean_product = jnp.mean(scaled * normed, axis=-1, keepdims=True)
    grad_values = inverse * (scaled - mean_scaled - normed * mean_product)
    return (grad_values, jnp.sum(grad_normed * normed, axis=0))


def rotary_tables(length):
    half_dim = HEAD_DIM // 2
    freqs = jnp.exp(jnp.arange(half_dim, dtype=jnp.float32) * (-math.log(10000.0) / half_dim))
    angles = jnp.arange(length, dtype=jnp.float32)[:, None] * freqs[None, :]
    return (jnp.cos(angles)[:, None, :], jnp.sin(angles)[:, None, :])


def rotate(values, rot_cos, rot_sin):
    half_dim = HEAD_DIM // 2
    lower = values[..., :half_dim]
    upper = values[..., half_dim:]
    return jnp.concatenate(
        [lower * rot_cos - upper * rot_sin, upper * rot_cos + lower * rot_sin], axis=-1
    )


def rotate_back(values, rot_cos, rot_sin):
    half_dim = HEAD_DIM // 2
    lower = values[..., :half_dim]
    upper = values[..., half_dim:]
    return jnp.concatenate(
        [lower * rot_cos + upper * rot_sin, upper * rot_cos - lower * rot_sin], axis=-1
    )


def attend_forward(queries, keys_in, values_in):
    scale_factor = HEAD_DIM ** (-0.5)
    scores = (
        jnp.einsum("qhd,khd->hqk", queries, keys_in, preferred_element_type=jnp.float32)
        * scale_factor
    )
    row_max = jnp.max(scores, axis=-1, keepdims=True)
    shifted = jnp.exp(scores - row_max)
    row_total = jnp.sum(shifted, axis=-1, keepdims=True)
    soft_probs = (shifted / row_total).astype(jnp.bfloat16)
    mixed = jnp.einsum("hqk,khd->qhd", soft_probs, values_in, preferred_element_type=jnp.float32)
    return (mixed, row_max + jnp.log(row_total))


def attend_back(queries, keys_in, values_in, log_total, grad_mixed):
    scale_factor = HEAD_DIM ** (-0.5)
    scores = (
        jnp.einsum("qhd,khd->hqk", queries, keys_in, preferred_element_type=jnp.float32)
        * scale_factor
    )
    soft_probs = jnp.exp(scores - log_total)
    grad_values = jnp.einsum(
        "hqk,qhd->khd",
        soft_probs.astype(jnp.bfloat16),
        grad_mixed,
        preferred_element_type=jnp.float32,
    )
    grad_probs = jnp.einsum(
        "qhd,khd->hqk", grad_mixed, values_in, preferred_element_type=jnp.float32
    )
    weighted = jnp.sum(soft_probs * grad_probs, axis=-1, keepdims=True)
    grad_scores = (soft_probs * (grad_probs - weighted)).astype(jnp.bfloat16)
    grad_queries = (
        jnp.einsum("hqk,khd->qhd", grad_scores, keys_in, preferred_element_type=jnp.float32)
        * scale_factor
    )
    grad_keys = (
        jnp.einsum("hqk,qhd->khd", grad_scores, queries, preferred_element_type=jnp.float32)
        * scale_factor
    )
    return (grad_queries, grad_keys, grad_values)


def body(
    x_input,
    cond_tokens,
    teacher,
    valid_mask,
    norm_gains,
    w_query,
    w_key,
    w_value,
    w_out,
    c_query,
    c_key,
    c_value,
    c_out,
    w_gate,
    w_up,
    w_down,
):
    bf_type = jnp.bfloat16

    def fetch_attention():
        return (
            lax.all_gather(w_query, "dp", axis=0, tiled=True),
            lax.all_gather(w_key, "dp", axis=0, tiled=True),
            lax.all_gather(w_value, "dp", axis=0, tiled=True),
            lax.all_gather(w_out, "dp", axis=1, tiled=True),
            lax.all_gather(c_query, "dp", axis=0, tiled=True),
            lax.all_gather(c_key, "dp", axis=0, tiled=True),
            lax.all_gather(c_value, "dp", axis=0, tiled=True),
            lax.all_gather(c_out, "dp", axis=1, tiled=True),
            lax.all_gather(norm_gains, "dp", axis=1, tiled=True),
        )

    def fetch_mlp():
        return (
            lax.all_gather(w_gate, "dp", axis=0, tiled=True),
            lax.all_gather(w_up, "dp", axis=0, tiled=True),
            lax.all_gather(w_down, "dp", axis=1, tiled=True),
        )

    def gather_rows(values):
        return lax.all_gather(values, "tensor", axis=0, tiled=True)

    def scatter_rows(values):
        return lax.psum_scatter(values, "tensor", scatter_dimension=0, tiled=True)

    def gather_grads(values):
        return lax.all_gather(values, "tensor", axis=0, tiled=True)

    def scatter_grads(values):
        return lax.psum_scatter(values, "tensor", scatter_dimension=0, tiled=True)

    local_rows = x_input[0].astype(jnp.float32)
    cond_rows = cond_tokens[0]
    mask_float = valid_mask[0].astype(jnp.float32)
    width = local_rows.shape[1]
    token_total = float(lax.axis_size("dp") * lax.axis_size("tensor") * local_rows.shape[0])
    weight_q, weight_k, weight_v, weight_o, cross_q, cross_k, cross_v, cross_o, gains_bf = (
        fetch_attention()
    )
    gains = gains_bf.astype(jnp.float32)
    normed_one, inverse_one = norm_stats(local_rows)
    input_one = gather_rows((normed_one * gains[0]).astype(bf_type))
    length = input_one.shape[0]
    ctx_len = cond_rows.shape[0]
    rot_cos, rot_sin = rotary_tables(length)
    query_rot = rotate(
        matmul(input_one, weight_q).reshape(length, -1, HEAD_DIM), rot_cos, rot_sin
    ).astype(bf_type)
    key_rot = rotate(
        matmul(input_one, weight_k).reshape(length, -1, HEAD_DIM), rot_cos, rot_sin
    ).astype(bf_type)
    value_self = matmul(input_one, weight_v).astype(bf_type).reshape(length, -1, HEAD_DIM)
    mixed_self, log_self = attend_forward(query_rot, key_rot, value_self)
    mixed_self = mixed_self.reshape(length, -1).astype(bf_type)
    hidden_one = local_rows + scatter_rows(matmul(mixed_self, weight_o))
    normed_two, inverse_two = norm_stats(hidden_one)
    input_two = gather_rows((normed_two * gains[1]).astype(bf_type))
    query_cross = matmul(input_two, cross_q).astype(bf_type).reshape(length, -1, HEAD_DIM)
    key_cross = matmul(cond_rows, cross_k).astype(bf_type).reshape(ctx_len, -1, HEAD_DIM)
    value_cross = matmul(cond_rows, cross_v).astype(bf_type).reshape(ctx_len, -1, HEAD_DIM)
    mixed_cross, log_cross = attend_forward(query_cross, key_cross, value_cross)
    mixed_cross = mixed_cross.reshape(length, -1).astype(bf_type)
    hidden_two = hidden_one + scatter_rows(matmul(mixed_cross, cross_o))
    weight_gate, weight_up, weight_down = fetch_mlp()
    normed_three, inverse_three = norm_stats(hidden_two)
    input_three = gather_rows((normed_three * gains[2]).astype(bf_type))
    gate_pre = matmul(input_three, weight_gate)
    up_pre = matmul(input_three, weight_up)
    gate_sigmoid = jax.nn.sigmoid(gate_pre)
    gate_silu = gate_pre * gate_sigmoid
    hidden_ff = (gate_silu * up_pre).astype(bf_type)
    block_out = hidden_two + scatter_rows(matmul(hidden_ff, weight_down))
    error_diff = block_out - teacher[0].astype(jnp.float32)
    local_error = jnp.sum(mask_float[:, None] * error_diff * error_diff)
    valid_count, error_total = lax.psum((jnp.sum(mask_float), local_error), ("dp", "tensor"))
    mean_loss = error_total / (width * valid_count)
    grad_out = 2.0 * token_total / valid_count * mask_float[:, None] * error_diff
    weight_gate, weight_up, weight_down = fetch_mlp()
    branch_three = gather_grads(grad_out.astype(bf_type))
    grad_hidden = times_transposed(branch_three, weight_down)
    grad_down = contract_rows(hidden_ff, branch_three)
    grad_gate = (
        grad_hidden * up_pre * gate_sigmoid * (1.0 + gate_pre * (1.0 - gate_sigmoid))
    ).astype(bf_type)
    grad_upper = (grad_hidden * gate_silu).astype(bf_type)
    grad_gate_w = contract_rows(input_three, grad_gate)
    grad_up_w = contract_rows(input_three, grad_upper)
    grad_normed_three = scatter_grads(
        times_transposed(grad_gate, weight_gate) + times_transposed(grad_upper, weight_up)
    )
    grad_gate_s, grad_up_s, grad_down_s = (
        lax.psum_scatter(grad_gate_w, "dp", scatter_dimension=0, tiled=True),
        lax.psum_scatter(grad_up_w, "dp", scatter_dimension=0, tiled=True),
        lax.psum_scatter(grad_down, "dp", scatter_dimension=1, tiled=True),
    )
    back_three, gain_three = norm_back(grad_normed_three, normed_three, inverse_three, gains[2])
    grad_two = grad_out + back_three
    weight_q, weight_k, weight_v, weight_o, cross_q, cross_k, cross_v, cross_o, spare_gains = (
        fetch_attention()
    )
    branch_two = gather_grads(grad_two.astype(bf_type))
    grad_cross_o = contract_rows(mixed_cross, branch_two)
    grad_mixed_cross = (
        times_transposed(branch_two, cross_o).astype(bf_type).reshape(length, -1, HEAD_DIM)
    )
    grad_qc, grad_kc, grad_vc = attend_back(
        query_cross, key_cross, value_cross, log_cross, grad_mixed_cross
    )
    grad_qc = grad_qc.reshape(length, -1).astype(bf_type)
    grad_kc = grad_kc.reshape(ctx_len, -1).astype(bf_type)
    grad_vc = grad_vc.reshape(ctx_len, -1).astype(bf_type)
    grad_cross_q = contract_rows(input_two, grad_qc)
    grad_cross_k = contract_rows(cond_rows, grad_kc)
    grad_cross_v = contract_rows(cond_rows, grad_vc)
    cond_part = times_transposed(grad_kc, cross_k) + times_transposed(grad_vc, cross_v)
    grad_normed_two = scatter_grads(times_transposed(grad_qc, cross_q))
    back_two, gain_two = norm_back(grad_normed_two, normed_two, inverse_two, gains[1])
    grad_one = grad_two + back_two
    branch_one = gather_grads(grad_one.astype(bf_type))
    grad_self_o = contract_rows(mixed_self, branch_one)
    grad_mixed_self = (
        times_transposed(branch_one, weight_o).astype(bf_type).reshape(length, -1, HEAD_DIM)
    )
    grad_qs, grad_ks, grad_vs = attend_back(
        query_rot, key_rot, value_self, log_self, grad_mixed_self
    )
    grad_qs = rotate_back(grad_qs, rot_cos, rot_sin).reshape(length, -1).astype(bf_type)
    grad_ks = rotate_back(grad_ks, rot_cos, rot_sin).reshape(length, -1).astype(bf_type)
    grad_vs = grad_vs.reshape(length, -1).astype(bf_type)
    grad_self_q = contract_rows(input_one, grad_qs)
    grad_self_k = contract_rows(input_one, grad_ks)
    grad_self_v = contract_rows(input_one, grad_vs)
    grad_normed_one = scatter_grads(
        times_transposed(grad_qs, weight_q)
        + times_transposed(grad_ks, weight_k)
        + times_transposed(grad_vs, weight_v)
    )
    back_one, gain_one = norm_back(grad_normed_one, normed_one, inverse_one, gains[0])
    grad_rows = grad_one + back_one
    gain_part = jnp.stack([gain_one, gain_two, gain_three])
    cond_sum, gain_sum = (
        lax.psum(cond_part.astype(jnp.bfloat16), "tensor").astype(jnp.float32),
        lax.psum(gain_part.astype(jnp.bfloat16), "tensor").astype(jnp.float32),
    )
    (
        grad_q_s,
        grad_k_s,
        grad_v_s,
        grad_o_s,
        grad_cq_s,
        grad_ck_s,
        grad_cv_s,
        grad_co_s,
        grad_gain_s,
    ) = (
        lax.psum_scatter(grad_self_q, "dp", scatter_dimension=0, tiled=True),
        lax.psum_scatter(grad_self_k, "dp", scatter_dimension=0, tiled=True),
        lax.psum_scatter(grad_self_v, "dp", scatter_dimension=0, tiled=True),
        lax.psum_scatter(grad_self_o, "dp", scatter_dimension=1, tiled=True),
        lax.psum_scatter(grad_cross_q, "dp", scatter_dimension=0, tiled=True),
        lax.psum_scatter(grad_cross_k, "dp", scatter_dimension=0, tiled=True),
        lax.psum_scatter(grad_cross_v, "dp", scatter_dimension=0, tiled=True),
        lax.psum_scatter(grad_cross_o, "dp", scatter_dimension=1, tiled=True),
        lax.psum_scatter(gain_sum, "dp", scatter_dimension=1, tiled=True),
    )
    return (
        block_out.astype(bf_type)[None],
        mean_loss,
        grad_rows[None],
        cond_sum[None],
        grad_q_s,
        grad_k_s,
        grad_v_s,
        grad_o_s,
        grad_cq_s,
        grad_ck_s,
        grad_cv_s,
        grad_co_s,
        grad_gate_s,
        grad_up_s,
        grad_down_s,
        grad_gain_s,
    )


def solution(mesh):
    return jax.shard_map(
        body,
        mesh=mesh,
        in_specs=(
            P("dp", "tensor", None),
            P("dp", None, None),
            P("dp", "tensor", None),
            P("dp", "tensor"),
            P(None, "dp"),
            P("dp", "tensor"),
            P("dp", "tensor"),
            P("dp", "tensor"),
            P("tensor", "dp"),
            P("dp", "tensor"),
            P("dp", "tensor"),
            P("dp", "tensor"),
            P("tensor", "dp"),
            P("dp", "tensor"),
            P("dp", "tensor"),
            P("tensor", "dp"),
        ),
        out_specs=(
            P("dp", "tensor", None),
            P(),
            P("dp", "tensor", None),
            P("dp", None, None),
            P("dp", "tensor"),
            P("dp", "tensor"),
            P("dp", "tensor"),
            P("tensor", "dp"),
            P("dp", "tensor"),
            P("dp", "tensor"),
            P("dp", "tensor"),
            P("tensor", "dp"),
            P("dp", "tensor"),
            P("dp", "tensor"),
            P("tensor", "dp"),
            P(None, "dp"),
        ),
        check_vma=False,
    )
```

profile of v0, /device:TPU:0, one launch (start us, length us, event | category | flops | bytes accessed | tf_op | source)
XLA Modules:
  0.0 2735.1 jit_solution(5155967029090758559)
XLA Ops:
  69.5 44.6 %all-gather.25.cloned.1.call-done = bf16[1536,768]{1,0:T(8,128)(2,1)} async-done(((bf16[96,768]{1,0:T(8,128)(2,1)}), bf16[1536,768]{1,0:T(8,128)(2,1)}) %all-gather.25.cloned.1.call-update) | async-done | bytes 2359312 | tf_op jit(solution)/shard_map/all_gather | solution.py:134
  252.2 56.6 %reduce-scatter.25.cloned.1.call-done = f32[384,1536]{1,0:T(8,128)} async-done(((f32[768,1536]{1,0:T(8,128)}), f32[384,1536]{1,0:T(8,128)}) %reduce-scatter.25.cloned.1.call-update) | async-done | bytes 2359312 | tf_op jit(solution)/shard_map/reduce_scatter | solution.py:155
  314.0 39.8 %all-gather.29.cloned.1.call-done = bf16[1536,768]{1,0:T(8,128)(2,1)} async-done(((bf16[96,768]{1,0:T(8,128)(2,1)}), bf16[1536,768]{1,0:T(8,128)(2,1)}) %all-gather.29.cloned.1.call-update) | async-done | bytes 2359312 | tf_op jit(solution)/shard_map/all_gather | solution.py:139
  356.9 40.6 %all-gather.35.cloned.1.call-done = bf16[1536,768]{1,0:T(8,128)(2,1)} async-done(((bf16[96,768]{1,0:T(8,128)(2,1)}), bf16[1536,768]{1,0:T(8,128)(2,1)}) %all-gather.35.cloned.1.call-update) | async-done | bytes 2359312 | tf_op jit(solution)/shard_map/all_gather | solution.py:138
  399.8 41.3 %all-gather.33.cloned.1.call-done = bf16[1536,768]{1,0:T(8,128)(2,1)} async-done(((bf16[96,768]{1,0:T(8,128)(2,1)}), bf16[1536,768]{1,0:T(8,128)(2,1)}) %all-gather.33.cloned.1.call-update) | async-done | bytes 2359312 | tf_op jit(solution)/shard_map/all_gather | solution.py:137
  530.0 58.1 %reduce-scatter.27.cloned.1.call-done = f32[384,1536]{1,0:T(8,128)} async-done(((f32[768,1536]{1,0:T(8,128)}), f32[384,1536]{1,0:T(8,128)}) %reduce-scatter.27.cloned.1.call-update) | async-done | bytes 2359312 | tf_op jit(solution)/shard_map/reduce_scatter | solution.py:155
  594.5 77.3 %all-gather.41.cloned.1.call-done = bf16[1536,3072]{1,0:T(8,128)(2,1)} async-done(((bf16[96,3072]{1,0:T(8,128)(2,1)}), bf16[1536,3072]{1,0:T(8,128)(2,1)}) %all-gather.41.cloned.1.call-update) | async-done | bytes 9437200 | tf_op jit(solution)/shard_map/all_gather | solution.py:146
  722.2 69.5 %all-gather.43.cloned.1.call-done = bf16[1536,3072]{1,0:T(8,128)(2,1)} async-done(((bf16[96,3072]{1,0:T(8,128)(2,1)}), bf16[1536,3072]{1,0:T(8,128)(2,1)}) %all-gather.43.cloned.1.call-update) | async-done | bytes 9437200 | tf_op jit(solution)/shard_map/all_gather | solution.py:147
  808.0 65.4 %all-gather.45.cloned.1.call-done = bf16[3072,1536]{0,1:T(8,128)(2,1)} async-done(((bf16[3072,96]{0,1:T(8,128)(2,1)}), bf16[3072,1536]{0,1:T(8,128)(2,1)}) %all-gather.45.cloned.1.call-update) | async-done | bytes 9437200 | tf_op jit(solution)/shard_map/all_gather | solution.py:148
  887.7 39.0 %psum.29 = f32[]{:T(128)} all-reduce(f32[]{:T(128)} %get-tuple-element.93), channel_id=1, replica_groups=mesh['dp'=16,'tensor'=2] {'dp','tensor'}, use_global_device_ids=true, to_apply=%region_16.0 | all-reduce | flops 1 | bytes 8 | tf_op jit(solution)/shard_map/psum | solution.py:206
  1029.3 60.1 %reduce-scatter.31.cloned.1.call-done = f32[384,1536]{1,0:T(8,128)} async-done(((f32[768,1536]{1,0:T(8,128)}), f32[384,1536]{1,0:T(8,128)}) %reduce-scatter.31.cloned.1.call-update) | async-done | bytes 2359312 | tf_op jit(solution)/shard_map/reduce_scatter | solution.py:161
  1151.6 60.1 %reduce-scatter.33.cloned.1.call-done = f32[384,1536]{1,0:T(8,128)} async-done(((f32[768,1536]{1,0:T(8,128)}), f32[384,1536]{1,0:T(8,128)}) %reduce-scatter.33.cloned.1.call-update) | async-done | bytes 2359312 | tf_op jit(solution)/shard_map/reduce_scatter | solution.py:161
  1356.9 48.8 %reduce-scatter.35.cloned.1.call-done = f32[384,1536]{1,0:T(8,128)} async-done(((f32[768,1536]{1,0:T(8,128)}), f32[384,1536]{1,0:T(8,128)}) %reduce-scatter.35.cloned.1.call-update) | async-done | bytes 2359312 | tf_op jit(solution)/shard_map/reduce_scatter | solution.py:161
  1519.5 42.2 %psum.28 = f32[]{:T(128)} all-reduce(f32[]{:T(128)} %get-tuple-element.89), channel_id=1, replica_groups=mesh['dp'=16,'tensor'=2] {'dp','tensor'}, use_global_device_ids=true, to_apply=%region_14.0 | all-reduce | flops 1 | bytes 8 | tf_op jit(solution)/shard_map/psum | solution.py:206
  1575.0 78.9 %reduce-scatter.45.cloned.1.call-done = f32[96,768]{1,0:T(8,128)} async-done(((f32[1536,768]{1,0:T(8,128)}), f32[96,768]{1,0:T(8,128)}) %reduce-scatter.45.cloned.1.call-update) | async-done | bytes 294928 | tf_op jit(solution)/shard_map/reduce_scatter | solution.py:291
  1653.9 79.6 %reduce-scatter.57.cloned.1.call-done = f32[96,768]{1,0:T(8,128)} async-done(((f32[1536,768]{1,0:T(8,128)}), f32[96,768]{1,0:T(8,128)}) %reduce-scatter.57.cloned.1.call-update) | async-done | bytes 294928
  1733.5 79.1 %reduce-scatter.55.cloned.1.call-done = f32[96,768]{1,0:T(8,128)} async-done(((f32[1536,768]{1,0:T(8,128)}), f32[96,768]{1,0:T(8,128)}) %reduce-scatter.55.cloned.1.call-update) | async-done | bytes 294928
  1812.6 198.9 %reduce-scatter.53.cloned.1.call-done = f32[3072,96]{0,1:T(8,128)} async-done(((f32[3072,1536]{0,1:T(8,128)}), f32[3072,96]{0,1:T(8,128)}) %reduce-scatter.53.cloned.1.call-update) | async-done | bytes 1179664 | tf_op jit(solution)/shard_map/reduce_scatter | solution.py:225
  2011.5 199.2 %reduce-scatter.51.cloned.1.call-done = f32[96,3072]{1,0:T(8,128)} async-done(((f32[1536,3072]{1,0:T(8,128)}), f32[96,3072]{1,0:T(8,128)}) %reduce-scatter.51.cloned.1.call-update) | async-done | bytes 1179664 | tf_op jit(solution)/shard_map/reduce_scatter | solution.py:224
  2210.7 199.3 %reduce-scatter.49.cloned.1.call-done = f32[96,3072]{1,0:T(8,128)} async-done(((f32[1536,3072]{1,0:T(8,128)}), f32[96,3072]{1,0:T(8,128)}) %reduce-scatter.49.cloned.1.call-update) | async-done | bytes 1179664 | tf_op jit(solution)/shard_map/reduce_scatter | solution.py:223
  2410.0 79.5 %reduce-scatter.43.cloned.1.call-done = f32[768,96]{0,1:T(8,128)} async-done(((f32[768,1536]{0,1:T(8,128)}), f32[768,96]{0,1:T(8,128)}) %reduce-scatter.43.cloned.1.call-update) | async-done | bytes 294928 | tf_op jit(solution)/shard_map/reduce_scatter | solution.py:290
  2489.5 79.1 %reduce-scatter.41.cloned.1.call-done = f32[96,768]{1,0:T(8,128)} async-done(((f32[1536,768]{1,0:T(8,128)}), f32[96,768]{1,0:T(8,128)}) %reduce-scatter.41.cloned.1.call-update) | async-done | bytes 294928 | tf_op jit(solution)/shard_map/reduce_scatter | solution.py:289
  2568.5 79.6 %reduce-scatter.39.cloned.1.call-done = f32[96,768]{1,0:T(8,128)} async-done(((f32[1536,768]{1,0:T(8,128)}), f32[96,768]{1,0:T(8,128)}) %reduce-scatter.39.cloned.1.call-update) | async-done | bytes 294928 | tf_op jit(solution)/shard_map/reduce_scatter | solution.py:288
  2648.1 78.9 %reduce-scatter.37.cloned.1.call-done = f32[96,768]{1,0:T(8,128)} async-done(((f32[1536,768]{1,0:T(8,128)}), f32[96,768]{1,0:T(8,128)}) %reduce-scatter.37.cloned.1.call-update) | async-done | bytes 294928 | tf_op jit(solution)/shard_map/reduce_scatter | solution.py:287
  (342 shorter events, 820.7 us)
Async XLA Ops:
  37.4 163.4 %all-gather.21.cloned.1.call-start = ((), (), s32[]{:S(2)}) async-start(), calls=%async_computation.19 | async-start | bytes 2506752 | tf_op jit(solution)/shard_map/all_gather | solution.py:135
  38.0 206.1 %all-gather.27.cloned.1.call-start = ((), (), s32[]{:S(2)}) async-start(), calls=%async_computation.22 | async-start | bytes 2506752 | tf_op jit(solution)/shard_map/all_gather | solution.py:136
  38.6 270.3 %reduce-scatter.25.cloned.1.call-start = ((), (), s32[]{:S(2)}) async-start(), calls=%async_computation.23 | async-start | bytes 7077888 | tf_op jit(solution)/shard_map/reduce_scatter | solution.py:155
  251.5 189.7 %all-gather.33.cloned.1.call-start = ((), (), s32[]{:S(2)}) async-start(), calls=%async_computation.26 | async-start | bytes 2506752 | tf_op jit(solution)/shard_map/all_gather | solution.py:137
  252.2 225.9 %all-gather.31.cloned.1.call-start = ((), (), s32[]{:S(2)}) async-start(), calls=%async_computation.25 | async-start | bytes 3538944 | tf_op jit(solution)/shard_map/all_gather | solution.py:152
  313.0 209.9 %all-gather.37.cloned.1.call-start = ((), (), s32[]{:S(2)}) async-start(), calls=%async_computation.28 | async-start | bytes 2506752 | tf_op jit(solution)/shard_map/all_gather | solution.py:140
  313.8 274.3 %reduce-scatter.27.cloned.1.call-start = ((), (), s32[]{:S(2)}) async-start(), calls=%async_computation.29 | async-start | bytes 7077888 | tf_op jit(solution)/shard_map/reduce_scatter | solution.py:155
  529.9 178.2 %all-gather.39.cloned.1.call-start = ((), (), s32[]{:S(2)}) async-start(), calls=%async_computation.30 | async-start | bytes 3538944 | tf_op jit(solution)/shard_map/all_gather | solution.py:152
  593.1 198.6 %all-gather.43.cloned.1.call-start = ((), (), s32[]{:S(2)}) async-start(), calls=%async_computation.32 | async-start | bytes 10027008 | tf_op jit(solution)/shard_map/all_gather | solution.py:147
  593.7 279.7 %all-gather.45.cloned.1.call-start = ((), (), s32[]{:S(2)}) async-start(), calls=%async_computation.33 | async-start | bytes 10027008 | tf_op jit(solution)/shard_map/all_gather | solution.py:148
  594.3 351.8 %reduce-scatter.29.cloned.1.call-start = ((), (), s32[]{:S(2)}) async-start(), calls=%async_computation.34 | async-start | bytes 7077888 | tf_op jit(solution)/shard_map/reduce_scatter | solution.py:155
  1217.5 188.2 %reduce-scatter.35.cloned.1.call-start = ((), (), s32[]{:S(2)}) async-start(), calls=%async_computation.40 | async-start | bytes 7077888 | tf_op jit(solution)/shard_map/reduce_scatter | solution.py:161
  1345.6 216.8 %all-reduce.2.cloned.1.call-start = ((), (), s32[]{:S(2)}) async-start(), calls=%async_computation.41 | async-start | bytes 835584 | tf_op jit(solution)/shard_map/psum | solution.py:273
  1356.9 212.6 %reduce-scatter.59.cloned.1.call-start = ((), (), s32[]{:S(2)}) async-start(), calls=%async_computation.53 | async-start | bytes 835584
  1422.8 231.1 %reduce-scatter.45.cloned.1.call-start = ((), (), s32[]{:S(2)}) async-start(), calls=%async_computation.46 | async-start | bytes 5013504 | tf_op jit(solution)/shard_map/reduce_scatter | solution.py:291
  1429.0 304.5 %reduce-scatter.57.cloned.1.call-start = ((), (), s32[]{:S(2)}) async-start(), calls=%async_computation.52 | async-start | bytes 5013504
  1438.0 374.6 %reduce-scatter.55.cloned.1.call-start = ((), (), s32[]{:S(2)}) async-start(), calls=%async_computation.51 | async-start | bytes 5013504
  1447.3 564.2 %reduce-scatter.53.cloned.1.call-start = ((), (), s32[]{:S(2)}) async-start(), calls=%async_computation.50 | async-start | bytes 20054016 | tf_op jit(solution)/shard_map/reduce_scatter | solution.py:225
  1461.8 748.9 %reduce-scatter.51.cloned.1.call-start = ((), (), s32[]{:S(2)}) async-start(), calls=%async_computation.49 | async-start | bytes 20054016 | tf_op jit(solution)/shard_map/reduce_scatter | solution.py:224
  1475.7 934.3 %reduce-scatter.49.cloned.1.call-start = ((), (), s32[]{:S(2)}) async-start(), calls=%async_computation.48 | async-start | bytes 20054016 | tf_op jit(solution)/shard_map/reduce_scatter | solution.py:223
  1489.7 999.8 %reduce-scatter.43.cloned.1.call-start = ((), (), s32[]{:S(2)}) async-start(), calls=%async_computation.45 | async-start | bytes 5013504 | tf_op jit(solution)/shard_map/reduce_scatter | solution.py:290
  1497.0 1071.5 %reduce-scatter.41.cloned.1.call-start = ((), (), s32[]{:S(2)}) async-start(), calls=%async_computation.44 | async-start | bytes 5013504 | tf_op jit(solution)/shard_map/reduce_scatter | solution.py:289
  1504.2 1143.9 %reduce-scatter.39.cloned.1.call-start = ((), (), s32[]{:S(2)}) async-start(), calls=%async_computation.43 | async-start | bytes 5013504 | tf_op jit(solution)/shard_map/reduce_scatter | solution.py:288
  1511.5 1215.5 %reduce-scatter.37.cloned.1.call-start = ((), (), s32[]{:S(2)}) async-start(), calls=%async_computation.42 | async-start | bytes 5013504 | tf_op jit(solution)/shard_map/reduce_scatter | solution.py:287
  (88 other events, 3885.3 us)
Sparse Core Ops, SparseCore 0:
  71.7 42.3 all-gather.24
  250.1 58.7 reduce-scatter.24
  311.4 42.3 all-gather.28
  480.6 42.3 all-gather.36
  529.3 58.7 reduce-scatter.26
  590.4 81.4 all-gather.40
  710.2 81.4 all-gather.42
  793.8 79.5 all-gather.44
  886.5 59.5 reduce-scatter.28
  1029.4 59.9 reduce-scatter.30
  1151.6 59.9 reduce-scatter.32
  1345.7 59.9 reduce-scatter.34
  1438.3 56.7 reduce-scatter.58
  1499.8 75.1 reduce-scatter.46
  1579.3 74.5 reduce-scatter.44
  1658.8 74.6 reduce-scatter.56
  1737.9 74.6 reduce-scatter.54
  1817.7 193.8 reduce-scatter.52
  2016.8 193.8 reduce-scatter.50
  2215.9 194.0 reduce-scatter.48
  2414.8 74.6 reduce-scatter.42
  2493.9 74.5 reduce-scatter.40
  2573.5 74.5 reduce-scatter.38
  2652.4 74.5 reduce-scatter.36
  (12 shorter events, 441.5 us)
where the time goes:
time: 2740 us
  waiting for transfers between devices  2170 us (79%)
  matrix products  319 us (12%)
  blocking collectives  111 us (4%)
  other arithmetic  78.4 us (3%)
  local copies, waits for them, and re-layouts  35.4 us (1%)
    reduce_scatter x1, waiting for transfers between devices, body(): lax.psum_scatter(grad_gate_w, 'dp', scatter_dimension=0, tiled=True)  199 us
    reduce_scatter x1, waiting for transfers between devices, body(): lax.psum_scatter(grad_up_w, 'dp', scatter_dimension=0, tiled=True)  199 us
    reduce_scatter x1, waiting for transfers between devices, body(): lax.psum_scatter(grad_down, 'dp', scatter_dimension=1, tiled=True)  199 us
    reduce_scatter x3, waiting for transfers between devices, scatter_grads(): return lax.psum_scatter(values, 'tensor', scatter_dimension=0, tiled=True)  169 us
    unnamed x39, waiting for transfers between devices  166 us
    reduce_scatter x3, waiting for transfers between devices, scatter_rows(): return lax.psum_scatter(values, 'tensor', scatter_dimension=0, tiled=True)  133 us
    all_gather x3, waiting for transfers between devices, gather_grads(): return lax.all_gather(values, 'tensor', axis=0, tiled=True)  107 us
    all_gather x3, waiting for transfers between devices, gather_rows(): return lax.all_gather(values, 'tensor', axis=0, tiled=True)  103 us
  transfers between devices with their start and end apart: 36, of which 34 were waited for; matrix products, arithmetic and copies ran while one was open for 8% of the time, Pallas kernels for 0%

commit v1 on v0

--- a/solution.py
+++ b/solution.py
@@ -6,6 +6,27 @@
 
 HEAD_DIM = 64
 EPSILON = 1e-05
+
+
+def joined_along(pieces, dim):
+    pieces = jnp.moveaxis(pieces, 0, dim)
+    shape = pieces.shape
+    return pieces.reshape(*shape[:dim], shape[dim] * shape[dim + 1], *shape[dim + 2 :])
+
+
+def grow_blocks(shard, axis):
+    count, position = (lax.axis_size(axis), lax.axis_index(axis))
+    parts, bit = (shard[None], 1)
+    while bit < count:
+        theirs = lax.ppermute(parts, axis, [(i, i ^ bit) for i in range(count)])
+        low = position & bit == 0
+        parts = jnp.concatenate([jnp.where(low, parts, theirs), jnp.where(low, theirs, parts)])
+        bit *= 2
+    return parts
+
+
+def gather_by_bits(x, axis, dim):
+    return joined_along(grow_blocks(x, axis), dim)
 
 
 def matmul(left_side, right_side):
@@ -143,7 +164,7 @@
 
     def fetch_mlp():
         return (
-            lax.all_gather(w_gate, "dp", axis=0, tiled=True),
+            gather_by_bits(w_gate, "dp", 0),
             lax.all_gather(w_up, "dp", axis=0, tiled=True),
             lax.all_gather(w_down, "dp", axis=1, tiled=True),
         )

time: 2740 us -> 2900 us (1.058)
  waiting for transfers between devices: 2170 us -> 2310 us
    ppermute x0 -> x4, waiting for transfers between devices: none -> 384 us  [grow_blocks(): theirs = lax.ppermute(parts, axis, [(i, i ^ bit) for i in range(count)])]
    all_gather x1 -> x0, waiting for transfers between devices: 77.3 us -> none  [fetch_mlp(): lax.all_gather(w_gate, 'dp', axis=0, tiled=True)]
    all_gather x1, waiting for transfers between devices: 69.5 us -> 0.01 us  [fetch_mlp(): lax.all_gather(w_up, 'dp', axis=0, tiled=True)]
    all_gather x1, waiting for transfers between devices: 65.4 us -> 0.01 us  [fetch_mlp(): lax.all_gather(w_down, 'dp', axis=1, tiled=True)]
    all_gather x3, waiting for transfers between devices: 103 us -> 67.3 us  [gather_rows(): return lax.all_gather(values, 'tensor', axis=0, tiled=True)]
    unnamed x39 -> x38, waiting for transfers between devices: 166 us -> 165 us
  transfers between devices with their start and end apart: 36 -> 39, of which waited for: 34 -> 34; matrix products, arithmetic and copies ran while one was open for 8% -> 8% of each run, Pallas kernels for 0% -> 0%
where the time goes in v1:
time: 2900 us; the launch traced here: 2890 us
  waiting for transfers between devices  2310 us (80%)
  matrix products  318 us (11%)
  blocking collectives  111 us (4%)
  other arithmetic  92.7 us (3%)
  local copies, waits for them, and re-layouts  36.7 us (1%)
    ppermute x4, waiting for transfers between devices, grow_blocks(): theirs = lax.ppermute(parts, axis, [(i, i ^ bit) for i in range(count)])  384 us
    reduce_scatter x1, waiting for transfers between devices, body(): lax.psum_scatter(grad_gate_w, 'dp', scatter_dimension=0, tiled=True)  199 us
    reduce_scatter x1, waiting for transfers between devices, body(): lax.psum_scatter(grad_up_w, 'dp', scatter_dimension=0, tiled=True)  199 us
    reduce_scatter x1, waiting for transfers between devices, body(): lax.psum_scatter(grad_down, 'dp', scatter_dimension=1, tiled=True)  199 us
    reduce_scatter x3, waiting for transfers between devices, scatter_grads(): return lax.psum_scatter(values, 'tensor', scatter_dimension=0, tiled=True)  169 us
    unnamed x38, waiting for transfers between devices  165 us
    reduce_scatter x3, waiting for transfers between devices, scatter_rows(): return lax.psum_scatter(values, 'tensor', scatter_dimension=0, tiled=True)  136 us
    all_gather x3, waiting for transfers between devices, gather_grads(): return lax.all_gather(values, 'tensor', axis=0, tiled=True)  108 us
  transfers between devices with their start and end apart: 39, of which 34 were waited for; matrix products, arithmetic and copies ran while one was open for 8% of the time, Pallas kernels for 0%

profile of v1, /device:TPU:0, one launch (start us, length us, event | category | flops | bytes accessed | tf_op | source)
XLA Modules:
  0.0 2893.3 jit_solution(2558345846389660773)
XLA Ops:
  69.5 44.6 %all-gather.24.cloned.1.call-done = bf16[1536,768]{1,0:T(8,128)(2,1)} async-done(((bf16[96,768]{1,0:T(8,128)(2,1)}), bf16[1536,768]{1,0:T(8,128)(2,1)}) %all-gather.24.cloned.1.call-update) | async-done | bytes 2359312 | tf_op jit(solution)/shard_map/all_gather | solution.py:155
  118.6 38.9 %all-gather.22.cloned.1.call-done = bf16[1536,768]{1,0:T(8,128)(2,1)} async-done(((bf16[96,768]{1,0:T(8,128)(2,1)}), bf16[1536,768]{1,0:T(8,128)(2,1)}) %all-gather.22.cloned.1.call-update) | async-done | bytes 2359312 | tf_op jit(solution)/shard_map/all_gather | solution.py:154
  252.2 56.6 %reduce-scatter.25.cloned.1.call-done = f32[384,1536]{1,0:T(8,128)} async-done(((f32[768,1536]{1,0:T(8,128)}), f32[384,1536]{1,0:T(8,128)}) %reduce-scatter.25.cloned.1.call-update) | async-done | bytes 2359312 | tf_op jit(solution)/shard_map/reduce_scatter | solution.py:176
  314.0 39.7 %all-gather.28.cloned.1.call-done = bf16[1536,768]{1,0:T(8,128)(2,1)} async-done(((bf16[96,768]{1,0:T(8,128)(2,1)}), bf16[1536,768]{1,0:T(8,128)(2,1)}) %all-gather.28.cloned.1.call-update) | async-done | bytes 2359312 | tf_op jit(solution)/shard_map/all_gather | solution.py:160
  356.9 40.6 %all-gather.34.cloned.1.call-done = bf16[1536,768]{1,0:T(8,128)(2,1)} async-done(((bf16[96,768]{1,0:T(8,128)(2,1)}), bf16[1536,768]{1,0:T(8,128)(2,1)}) %all-gather.34.cloned.1.call-update) | async-done | bytes 2359312 | tf_op jit(solution)/shard_map/all_gather | solution.py:159
  399.8 41.3 %all-gather.32.cloned.1.call-done = bf16[1536,768]{1,0:T(8,128)(2,1)} async-done(((bf16[96,768]{1,0:T(8,128)(2,1)}), bf16[1536,768]{1,0:T(8,128)(2,1)}) %all-gather.32.cloned.1.call-update) | async-done | bytes 2359312 | tf_op jit(solution)/shard_map/all_gather | solution.py:158
  529.2 58.9 %reduce-scatter.27.cloned.1.call-done = f32[384,1536]{1,0:T(8,128)} async-done(((f32[768,1536]{1,0:T(8,128)}), f32[384,1536]{1,0:T(8,128)}) %reduce-scatter.27.cloned.1.call-update) | async-done | bytes 2359312 | tf_op jit(solution)/shard_map/reduce_scatter | solution.py:176
  628.3 98.6 %collective-permute-done.2 = bf16[4,96,3072]{2,1,0:T(8,128)(2,1)} collective-permute-done((bf16[4,96,3072]{2,1,0:T(8,128)(2,1)S(1)}, bf16[4,96,3072]{2,1,0:T(8,128)(2,1)}, u32[]{:S(2)}, u32[]{:S(2)}) %collective-permute-start.2) | collective-permute-done | bytes 2359328 | tf_op jit(solution)/shard_map/ppermute | solution.py:21
  736.3 257.4 %collective-permute-done.3 = bf16[8,96,3072]{2,1,0:T(8,128)(2,1)} collective-permute-done((bf16[8,96,3072]{2,1,0:T(8,128)(2,1)}, bf16[8,96,3072]{2,1,0:T(8,128)(2,1)}, u32[]{:S(2)}, u32[]{:S(2)}) %collective-permute-start.3) | collective-permute-done | bytes 4718624 | tf_op jit(solution)/shard_map/ppermute | solution.py:21
  1044.9 38.3 %psum.29 = f32[]{:T(128)} all-reduce(f32[]{:T(128)} %get-tuple-element.93), channel_id=1, replica_groups=mesh['dp'=16,'tensor'=2] {'dp','tensor'}, use_global_device_ids=true, to_apply=%region_16.17 | all-reduce | flops 1 | bytes 8 | tf_op jit(solution)/shard_map/psum | solution.py:227
  1187.5 60.1 %reduce-scatter.31.cloned.1.call-done = f32[384,1536]{1,0:T(8,128)} async-done(((f32[768,1536]{1,0:T(8,128)}), f32[384,1536]{1,0:T(8,128)}) %reduce-scatter.31.cloned.1.call-update) | async-done | bytes 2359312 | tf_op jit(solution)/shard_map/reduce_scatter | solution.py:182
  1309.7 60.1 %reduce-scatter.33.cloned.1.call-done = f32[384,1536]{1,0:T(8,128)} async-done(((f32[768,1536]{1,0:T(8,128)}), f32[384,1536]{1,0:T(8,128)}) %reduce-scatter.33.cloned.1.call-update) | async-done | bytes 2359312 | tf_op jit(solution)/shard_map/reduce_scatter | solution.py:182
  1515.1 48.8 %reduce-scatter.35.cloned.1.call-done = f32[384,1536]{1,0:T(8,128)} async-done(((f32[768,1536]{1,0:T(8,128)}), f32[384,1536]{1,0:T(8,128)}) %reduce-scatter.35.cloned.1.call-update) | async-done | bytes 2359312 | tf_op jit(solution)/shard_map/reduce_scatter | solution.py:182
  1677.7 42.2 %psum.28 = f32[]{:T(128)} all-reduce(f32[]{:T(128)} %get-tuple-element.89), channel_id=1, replica_groups=mesh['dp'=16,'tensor'=2] {'dp','tensor'}, use_global_device_ids=true, to_apply=%region_14.15 | all-reduce | flops 1 | bytes 8 | tf_op jit(solution)/shard_map/psum | solution.py:227
  1733.3 78.9 %reduce-scatter.45.cloned.1.call-done = f32[96,768]{1,0:T(8,128)} async-done(((f32[1536,768]{1,0:T(8,128)}), f32[96,768]{1,0:T(8,128)}) %reduce-scatter.45.cloned.1.call-update) | async-done | bytes 294928 | tf_op jit(solution)/shard_map/reduce_scatter | solution.py:312
  1812.2 79.4 %reduce-scatter.57.cloned.1.call-done = f32[96,768]{1,0:T(8,128)} async-done(((f32[1536,768]{1,0:T(8,128)}), f32[96,768]{1,0:T(8,128)}) %reduce-scatter.57.cloned.1.call-update) | async-done | bytes 294928
  1891.7 79.0 %reduce-scatter.55.cloned.1.call-done = f32[96,768]{1,0:T(8,128)} async-done(((f32[1536,768]{1,0:T(8,128)}), f32[96,768]{1,0:T(8,128)}) %reduce-scatter.55.cloned.1.call-update) | async-done | bytes 294928
  1970.7 199.1 %reduce-scatter.53.cloned.1.call-done = f32[3072,96]{0,1:T(8,128)} async-done(((f32[3072,1536]{0,1:T(8,128)}), f32[3072,96]{0,1:T(8,128)}) %reduce-scatter.53.cloned.1.call-update) | async-done | bytes 1179664 | tf_op jit(solution)/shard_map/reduce_scatter | solution.py:246
  2169.9 199.2 %reduce-scatter.49.cloned.1.call-done = f32[96,3072]{1,0:T(8,128)} async-done(((f32[1536,3072]{1,0:T(8,128)}), f32[96,3072]{1,0:T(8,128)}) %reduce-scatter.49.cloned.1.call-update) | async-done | bytes 1179664 | tf_op jit(solution)/shard_map/reduce_scatter | solution.py:244
  2369.0 199.2 %reduce-scatter.51.cloned.1.call-done = f32[96,3072]{1,0:T(8,128)} async-done(((f32[1536,3072]{1,0:T(8,128)}), f32[96,3072]{1,0:T(8,128)}) %reduce-scatter.51.cloned.1.call-update) | async-done | bytes 1179664 | tf_op jit(solution)/shard_map/reduce_scatter | solution.py:245
  2568.2 79.6 %reduce-scatter.43.cloned.1.call-done = f32[768,96]{0,1:T(8,128)} async-done(((f32[768,1536]{0,1:T(8,128)}), f32[768,96]{0,1:T(8,128)}) %reduce-scatter.43.cloned.1.call-update) | async-done | bytes 294928 | tf_op jit(solution)/shard_map/reduce_scatter | solution.py:311
  2647.8 78.9 %reduce-scatter.41.cloned.1.call-done = f32[96,768]{1,0:T(8,128)} async-done(((f32[1536,768]{1,0:T(8,128)}), f32[96,768]{1,0:T(8,128)}) %reduce-scatter.41.cloned.1.call-update) | async-done | bytes 294928 | tf_op jit(solution)/shard_map/reduce_scatter | solution.py:310
  2726.7 79.6 %reduce-scatter.39.cloned.1.call-done = f32[96,768]{1,0:T(8,128)} async-done(((f32[1536,768]{1,0:T(8,128)}), f32[96,768]{1,0:T(8,128)}) %reduce-scatter.39.cloned.1.call-update) | async-done | bytes 294928 | tf_op jit(solution)/shard_map/reduce_scatter | solution.py:309
  2806.4 79.0 %reduce-scatter.37.cloned.1.call-done = f32[96,768]{1,0:T(8,128)} async-done(((f32[1536,768]{1,0:T(8,128)}), f32[96,768]{1,0:T(8,128)}) %reduce-scatter.37.cloned.1.call-update) | async-done | bytes 294928 | tf_op jit(solution)/shard_map/reduce_scatter | solution.py:308
  (383 shorter events, 796.1 us)
Async XLA Ops:
  38.0 206.1 %all-gather.26.cloned.1.call-start = ((), (), s32[]{:S(2)}) async-start(), calls=%async_computation.22 | async-start | bytes 2506752 | tf_op jit(solution)/shard_map/all_gather | solution.py:157
  38.6 270.3 %reduce-scatter.25.cloned.1.call-start = ((), (), s32[]{:S(2)}) async-start(), calls=%async_computation.23 | async-start | bytes 7077888 | tf_op jit(solution)/shard_map/reduce_scatter | solution.py:176
  251.4 189.7 %all-gather.32.cloned.1.call-start = ((), (), s32[]{:S(2)}) async-start(), calls=%async_computation.26 | async-start | bytes 2506752 | tf_op jit(solution)/shard_map/all_gather | solution.py:158
  252.2 225.9 %all-gather.30.cloned.1.call-start = ((), (), s32[]{:S(2)}) async-start(), calls=%async_computation.25 | async-start | bytes 3538944 | tf_op jit(solution)/shard_map/all_gather | solution.py:173
  313.0 209.9 %all-gather.36.cloned.1.call-start = ((), (), s32[]{:S(2)}) async-start(), calls=%async_computation.28 | async-start | bytes 2506752 | tf_op jit(solution)/shard_map/all_gather | solution.py:161
  313.8 274.3 %reduce-scatter.27.cloned.1.call-start = ((), (), s32[]{:S(2)}) async-start(), calls=%async_computation.29 | async-start | bytes 7077888 | tf_op jit(solution)/shard_map/reduce_scatter | solution.py:176
  529.2 472.0 %all-gather.38.cloned.1.call-start = ((), (), s32[]{:S(2)}) async-start(), calls=%async_computation.30 | async-start | bytes 3538944 | tf_op jit(solution)/shard_map/all_gather | solution.py:173
  593.1 421.1 %all-gather.40.cloned.1.call-start = ((), (), s32[]{:S(2)}) async-start(), calls=%async_computation.31 | async-start | bytes 10027008 | tf_op jit(solution)/shard_map/all_gather | solution.py:168
  593.7 436.8 %all-gather.42.cloned.1.call-start = ((), (), s32[]{:S(2)}) async-start(), calls=%async_computation.32 | async-start | bytes 10027008 | tf_op jit(solution)/shard_map/all_gather | solution.py:169
  594.3 509.6 %reduce-scatter.29.cloned.1.call-start = ((), (), s32[]{:S(2)}) async-start(), calls=%async_computation.33 | async-start | bytes 7077888 | tf_op jit(solution)/shard_map/reduce_scatter | solution.py:176
  732.5 261.2 %collective-permute-start.3 = (bf16[8,96,3072]{2,1,0:T(8,128)(2,1)}, bf16[8,96,3072]{2,1,0:T(8,128)(2,1)}, u32[]{:S(2)}, u32[]{:S(2)}) collective-permute-start(bf16[8,96,3072]{2,1,0:T(8,128)(2,1)} %pad_maximum_fusion.1), channel_id=1, source_target_pairs={{0,16},{2,18},{4,20},{6,22},{8,24},{10,26},{12,28},{14,30},{16,0},... | collective-permute-start | bytes 14155784 | tf_op jit(solution)/shard_map/ppermute | solution.py:21
  1375.6 188.3 %reduce-scatter.35.cloned.1.call-start = ((), (), s32[]{:S(2)}) async-start(), calls=%async_computation.39 | async-start | bytes 7077888 | tf_op jit(solution)/shard_map/reduce_scatter | solution.py:182
  1503.7 216.9 %all-reduce.2.cloned.1.call-start = ((), (), s32[]{:S(2)}) async-start(), calls=%async_computation.40 | async-start | bytes 835584 | tf_op jit(solution)/shard_map/psum | solution.py:294
  1515.0 212.8 %reduce-scatter.59.cloned.1.call-start = ((), (), s32[]{:S(2)}) async-start(), calls=%async_computation.52 | async-start | bytes 835584
  1580.9 231.3 %reduce-scatter.45.cloned.1.call-start = ((), (), s32[]{:S(2)}) async-start(), calls=%async_computation.45 | async-start | bytes 5013504 | tf_op jit(solution)/shard_map/reduce_scatter | solution.py:312
  1587.1 304.5 %reduce-scatter.57.cloned.1.call-start = ((), (), s32[]{:S(2)}) async-start(), calls=%async_computation.51 | async-start | bytes 5013504
  1596.2 374.5 %reduce-scatter.55.cloned.1.call-start = ((), (), s32[]{:S(2)}) async-start(), calls=%async_computation.50 | async-start | bytes 5013504
  1605.5 564.4 %reduce-scatter.53.cloned.1.call-start = ((), (), s32[]{:S(2)}) async-start(), calls=%async_computation.49 | async-start | bytes 20054016 | tf_op jit(solution)/shard_map/reduce_scatter | solution.py:246
  1620.1 748.9 %reduce-scatter.49.cloned.1.call-start = ((), (), s32[]{:S(2)}) async-start(), calls=%async_computation.47 | async-start | bytes 20054016 | tf_op jit(solution)/shard_map/reduce_scatter | solution.py:244
  1634.1 934.1 %reduce-scatter.51.cloned.1.call-start = ((), (), s32[]{:S(2)}) async-start(), calls=%async_computation.48 | async-start | bytes 20054016 | tf_op jit(solution)/shard_map/reduce_scatter | solution.py:245
  1647.9 999.9 %reduce-scatter.43.cloned.1.call-start = ((), (), s32[]{:S(2)}) async-start(), calls=%async_computation.44 | async-start | bytes 5013504 | tf_op jit(solution)/shard_map/reduce_scatter | solution.py:311
  1655.2 1071.5 %reduce-scatter.41.cloned.1.call-start = ((), (), s32[]{:S(2)}) async-start(), calls=%async_computation.43 | async-start | bytes 5013504 | tf_op jit(solution)/shard_map/reduce_scatter | solution.py:310
  1662.4 1144.0 %reduce-scatter.39.cloned.1.call-start = ((), (), s32[]{:S(2)}) async-start(), calls=%async_computation.42 | async-start | bytes 5013504 | tf_op jit(solution)/shard_map/reduce_scatter | solution.py:309
  1669.8 1215.6 %reduce-scatter.37.cloned.1.call-start = ((), (), s32[]{:S(2)}) async-start(), calls=%async_computation.41 | async-start | bytes 5013504 | tf_op jit(solution)/shard_map/reduce_scatter | solution.py:308
  (105 other events, 4728.0 us)
Sparse Core Ops, SparseCore 0:
  71.7 42.3 all-gather.23
  116.4 41.0 all-gather.21
  250.1 58.7 reduce-scatter.24
  311.4 42.3 all-gather.27
  480.6 42.3 all-gather.35
  529.3 58.7 reduce-scatter.26
  631.5 109.6 all-gather.39
  743.3 191.0 all-gather.41
  1043.7 60.1 reduce-scatter.28
  1187.6 59.9 reduce-scatter.30
  1309.8 59.9 reduce-scatter.32
  1503.8 59.9 reduce-scatter.34
  1596.5 56.6 reduce-scatter.58
  1658.1 75.1 reduce-scatter.46
  1737.6 74.5 reduce-scatter.44
  1817.0 74.6 reduce-scatter.56
  1896.1 74.5 reduce-scatter.54
  1976.0 193.8 reduce-scatter.52
  2174.9 194.0 reduce-scatter.48
  2374.3 193.8 reduce-scatter.50
  2573.1 74.6 reduce-scatter.42
  2652.1 74.6 reduce-scatter.40
  2731.7 74.6 reduce-scatter.38
  2810.8 74.5 reduce-scatter.36
  (11 shorter events, 402.5 us)
